TPU v7x, 128 devices: a whole 4x4x4 slice. The times are simulated.
128 devices in a mesh: sec: 4 (over y), dp: 8 (over x_hi, z), mp: 4 (over x_lo, core).
Axes of the slice: x: 4 (x_hi: 2, x_lo: 2; x = x_hi * 2 + x_lo), y: 4, z: 4, core: 2. Of those that a mesh axis runs over, the one named last changes fastest.
Arguments:
- patches: bfloat16 [320, 5120], P('dp'), may hold values from -6 to 6
- ln_gain: bfloat16 [1280], replicated, may hold values from 0.099609375 to 1.8984375
- ln_shift: bfloat16 [1280], replicated, may hold values from -3 to 3
- w_in: bfloat16 [5120, 5120], P('dp', ('sec', 'mp')), may hold values from -0.078125 to 0.078125
- b_in: bfloat16 [5120], P(('sec', 'mp')), may hold values from -3 to 3
- w_out: bfloat16 [5120, 8192], P(('sec', 'mp'), 'dp'), may hold values from -0.125 to 0.125
- b_out: bfloat16 [8192], P(('sec', 'mp')), may hold values from -3 to 3
- place: int32 [320], P('dp'), may hold values from 0 to 255, as said below
- image_counts: int32 [8], P('dp'), may hold values from 1 to 40, 128 in all
- text_rows: bfloat16 [2048, 8192], P('dp', ('sec', 'mp')), may hold values from -6 to 6
- segments: int32 [8, 256], P('dp'), may hold values from 0 to 3, never falling along the last dimension, each value on 1 to 128 neighbouring positions
- norm_gain: bfloat16 [2, 8192], replicated, may hold values from 0.099609375 to 1.8984375
- q_weight: bfloat16 [2, 8192, 4096], P(None, None, ('sec', 'mp'))
- kv_weight: bfloat16 [2, 2, 512, 8192], P(None, None, ('sec', 'mp'))
- o_weight: bfloat16 [2, 4096, 8192], P(None, ('sec', 'mp')), may hold values from -0.125 to 0.125
- grad_rows: bfloat16 [320, 8192], P('dp'), may hold values from -6 to 6
Outputs:
- final_rows: float32 [2048, 8192], P('dp', ('sec', 'mp'))
- patch_grads: float32 [320, 5120], P('dp')
Inputs may be any that keep to these rules, and one draw needn't show every extreme that they name: `place`: each owner's 40 entries are distinct token positions of its own packed sequence; only an owner's first image_counts entries are used. `image_counts`: the counts sum to 8 * (16) over all owners.
All inputs are finite; a program needn't handle non-finite values. No bound on the sum of `image_counts` on one device may be relied on, other than what follows from the above.
Results may differ from a plain program's by a relative error of at most 0.0055.
Values may be sent and summed in bfloat16 or wider, within the bound.
A program may use at most 128 MiB of HBM per device.

v0:
```python
import math
import jax
import jax.numpy as jnp
from jax import lax
from jax.sharding import PartitionSpec as P

D = 8192
HEAD_DIM = 128
ln_eps = 1e-06
rms_eps = 1e-06
rope_base = 1000000.0


def group_norm(patch_rows, ln_gain, ln_shift):
    row_count = patch_rows.shape[0]
    grouped = patch_rows.astype(jnp.float32).reshape(row_count, -1, ln_gain.shape[0])
    center = grouped - jnp.mean(grouped, axis=-1, keepdims=True)
    spread = jnp.mean(center * center, axis=-1, keepdims=True)
    scaled = center * lax.rsqrt(spread + ln_eps) * ln_gain.astype(jnp.float32) + ln_shift.astype(
        jnp.float32
    )
    return scaled.reshape(row_count, -1)


def gelu_exact(values):
    return jax.nn.gelu(values, approximate=False)


def rotate(values, positions):
    head_depth = values.shape[-1]
    half_depth = head_depth // 2
    inv_freq = rope_base ** (-2.0 * jnp.arange(half_depth, dtype=jnp.float32) / head_depth)
    angles = positions[:, None] * inv_freq[None, :]
    cosine = jnp.cos(angles)[:, None, :]
    sine_part = jnp.sin(angles)[:, None, :]
    first_half = values[..., :half_depth]
    second = values[..., half_depth:]
    return jnp.concatenate(
        [first_half * cosine - second * sine_part, second * cosine + first_half * sine_part],
        axis=-1,
    )


def doc_mask(segment_ids):
    token_index = jnp.arange(segment_ids.shape[0], dtype=jnp.int32)
    same_doc = segment_ids[:, None] == segment_ids[None, :]
    allowed = same_doc & (token_index[None, :] <= token_index[:, None])
    positions = jnp.sum(allowed.astype(jnp.int32), axis=1) - 1
    return (allowed, positions.astype(jnp.float32))


def attend(normed, allowed, positions, q_local, kv_local):
    token_count = normed.shape[0]
    queries = jnp.dot(normed, q_local, preferred_element_type=jnp.float32).reshape(
        token_count, -1, HEAD_DIM
    )
    key_value = jnp.einsum("td,kcd->tkc", normed, kv_local, preferred_element_type=jnp.float32)
    key_value = lax.all_gather(key_value, "mp", axis=2, tiled=True)
    key_rows = rotate(key_value[:, 0:1, :], positions)[:, 0, :].astype(jnp.bfloat16)
    value_rows = key_value[:, 1, :].astype(jnp.bfloat16)
    queries = rotate(queries, positions).astype(jnp.bfloat16)
    scores = jnp.einsum("thd,sd->hts", queries, key_rows, preferred_element_type=jnp.float32) * (
        1.0 / math.sqrt(HEAD_DIM)
    )
    scores = jnp.where(allowed[None], scores, -jnp.inf)
    row_max = jnp.max(scores, axis=-1, keepdims=True)
    exp_scores = jnp.exp(scores - row_max)
    attn_weights = (exp_scores / jnp.sum(exp_scores, axis=-1, keepdims=True)).astype(jnp.bfloat16)
    attended = jnp.einsum(
        "hts,sd->thd", attn_weights, value_rows, preferred_element_type=jnp.float32
    )
    return attended.astype(jnp.bfloat16).reshape(token_count, -1)


def gather_features(rows_local):
    return lax.all_gather(rows_local, ("sec", "mp"), axis=1, tiled=True)


def section_features(rows_local, gain_row, allowed, positions, q_local, kv_local, o_local):
    share = rows_local.shape[1]
    square_sums = lax.psum(jnp.sum(rows_local * rows_local, axis=1), ("sec", "mp"))
    factor = lax.rsqrt(square_sums / D + rms_eps)
    gain_local = lax.dynamic_slice_in_dim(
        gain_row, lax.axis_index(("sec", "mp")) * share, share, 0
    ).astype(jnp.float32)
    normed_local = (rows_local * factor[:, None] * gain_local[None, :]).astype(jnp.bfloat16)
    normed = gather_features(normed_local)
    attended = attend(normed, allowed, positions, q_local, kv_local)
    summed = lax.psum_scatter(
        lax.dot_general(
            o_local, attended, (((0,), (1,)), ((), ())), preferred_element_type=jnp.float32
        ),
        ("sec", "mp"),
        scatter_dimension=0,
        tiled=True,
    )
    return rows_local + summed.T


def merger_front(patch_rows, ln_gain, ln_shift, w_in_full, b_in, w_out_full, b_out):
    normed = group_norm(patch_rows, ln_gain, ln_shift).astype(jnp.bfloat16)
    pre_act = jnp.dot(normed, w_in_full, preferred_element_type=jnp.float32) + b_in.astype(
        jnp.float32
    )
    hidden_units = gelu_exact(pre_act).astype(jnp.bfloat16)
    partial_out = jnp.dot(hidden_units, w_out_full, preferred_element_type=jnp.float32)
    merged = lax.psum_scatter(
        partial_out, ("sec", "mp"), scatter_dimension=1, tiled=True
    ) + b_out.astype(jnp.float32)
    return (merged.astype(jnp.bfloat16), pre_act)


def merger_back(patch_rows, pre_act, hidden_grads, ln_gain, ln_shift, w_in_full):
    _, pull_gelu = jax.vjp(gelu_exact, pre_act)
    pre_grads = pull_gelu(hidden_grads)[0].astype(jnp.bfloat16)
    normed_grads = lax.dot_general(
        pre_grads, w_in_full, (((1,), (1,)), ((), ())), preferred_element_type=jnp.float32
    )
    normed_grads = lax.psum(normed_grads, ("sec", "mp"))
    _, pull_norm = jax.vjp(
        lambda values: group_norm(values, ln_gain, ln_shift), patch_rows.astype(jnp.float32)
    )
    return pull_norm(normed_grads)[0]


def local(
    patches,
    ln_gain,
    ln_shift,
    w_in,
    b_in,
    w_out,
    b_out,
    place,
    image_counts,
    text_rows,
    segments,
    norm_gain,
    q_weight,
    kv_weight,
    o_weight,
    grad_rows,
):
    w_in_full, w_out_full = (
        lax.all_gather(w_in, "dp", axis=0, tiled=True),
        lax.all_gather(w_out, "dp", axis=1, tiled=True),
    )
    slot_count = patches.shape[0]
    tokens = text_rows.shape[0]
    slot_index = jnp.arange(slot_count, dtype=jnp.int32)
    live_slot = slot_index < image_counts[0]
    slot_grads = jnp.where(live_slot[:, None], grad_rows, jnp.zeros_like(grad_rows))
    hidden_grads = lax.dot_general(
        slot_grads, w_out_full, (((1,), (1,)), ((), ())), preferred_element_type=jnp.float32
    )
    merged_local, pre_act = merger_front(
        patches, ln_gain, ln_shift, w_in_full, b_in, w_out_full, b_out
    )
    patch_grads = merger_back(patches, pre_act, hidden_grads, ln_gain, ln_shift, w_in_full)
    token_index = jnp.arange(tokens, dtype=jnp.int32)
    select = (place[:, None] == token_index[None, :]) & live_slot[:, None]
    is_image = jnp.any(select, axis=0)
    picked = lax.dot_general(
        select.astype(jnp.bfloat16),
        merged_local,
        (((0,), (0,)), ((), ())),
        preferred_element_type=jnp.float32,
    )
    start_rows = jnp.where(is_image[:, None], picked, text_rows.astype(jnp.float32)).astype(
        jnp.bfloat16
    )
    allowed, positions = doc_mask(segments[0])
    layer_count = q_weight.shape[0]
    current = start_rows.astype(jnp.float32)
    for layer_index in range(layer_count):
        current = section_features(
            current,
            norm_gain[layer_index],
            allowed,
            positions,
            q_weight[layer_index],
            kv_weight[layer_index],
            o_weight[layer_index],
        )
    return (current, patch_grads)


def solution(mesh):
    in_specs = (
        P("dp", None),
        P(),
        P(),
        P("dp", ("sec", "mp")),
        P(("sec", "mp")),
        P(("sec", "mp"), "dp"),
        P(("sec", "mp")),
        P("dp"),
        P("dp"),
        P("dp", ("sec", "mp")),
        P("dp", None),
        P(),
        P(None, None, ("sec", "mp")),
        P(None, None, ("sec", "mp"), None),
        P(None, ("sec", "mp"), None),
        P("dp", None),
    )
    out_specs = (P("dp", ("sec", "mp")), P("dp", None))
    return jax.shard_map(local, mesh=mesh, in_specs=in_specs, out_specs=out_specs, check_vma=False)
```

profile of v0, /device:TPU:0, one launch (start us, length us, event | category | flops | bytes accessed | tf_op | source)
XLA Modules:
  0.0 707.5 jit_solution(7781813747117255810)
XLA Ops:
  8.7 1.4 reshape.223
  11.5 64.8 %all-gather.5.cloned.1.call-done = bf16[5120,320]{0,1:T(8,128)(2,1)} async-done(((bf16[640,320]{0,1:T(8,128)(2,1)}), bf16[5120,320]{0,1:T(8,128)(2,1)}) %all-gather.5.cloned.1.call-update) | async-done | bytes 3276816 | tf_op jit(solution)/shard_map/all_gather | solution.py:145
  76.3 3.0 convolution_add_fusion
  79.4 77.0 %all-gather.7.cloned.1.call-done = bf16[320,8192]{1,0:T(8,128)(2,1)} async-done(((bf16[320,1024]{1,0:T(8,128)(2,1)}), bf16[320,8192]{1,0:T(8,128)(2,1)}) %all-gather.7.cloned.1.call-update) | async-done | bytes 5242896 | tf_op jit(solution)/shard_map/all_gather | solution.py:146
  156.4 4.6 fusion.88
  162.0 60.0 %reduce-scatter.4.cloned.1.call-done = f32[40,512]{1,0:T(8,128)} async-done(((f32[40,8192]{1,0:T(8,128)}), f32[40,512]{1,0:T(8,128)}) %reduce-scatter.4.cloned.1.call-update) | async-done | bytes 81936 | tf_op jit(solution)/shard_map/reduce_scatter | solution.py:107
  222.0 1.4 multiply_reduce_fusion.3
  223.4 27.7 %psum.21 = f32[256]{0:T(256)S(1)} all-reduce(f32[256]{0:T(256)S(1)} %get-tuple-element.16), channel_id=1, replica_groups=mesh['sec'=4,'dp'=8,'mp'=4] {'sec','mp'}, use_global_device_ids=true, to_apply=%region_5.6 | all-reduce | flops 256 | bytes 2048 | tf_op jit(solution)/shard_map/psum | solution.py:81
  252.0 5.7 slice_bitcast_fusion.1
  257.8 6.4 copy.26
  264.8 23.3 %all-gather.9.cloned.1.call-done = bf16[256,8192]{1,0:T(8,128)(2,1)} async-done(((bf16[256,512]{1,0:T(8,128)(2,1)}), bf16[256,8192]{1,0:T(8,128)(2,1)}) %all-gather.9.cloned.1.call-update) | async-done | bytes 4194320 | tf_op jit(solution)/shard_map/all_gather | solution.py:76
  288.1 4.0 fusion.10
  292.1 5.8 all_gather.21
  298.3 3.5 fusion.8
  303.5 1.2 fusion.117
  304.7 1.6 convolution_convert_fusion.1
  306.3 6.7 convolution_bitcast_fusion.1
  313.1 97.8 %reduce-scatter.6.cloned.1.call-done = f32[512,256]{0,1:T(8,128)} async-done(((f32[8192,256]{0,1:T(8,128)}), f32[512,256]{0,1:T(8,128)}) %reduce-scatter.6.cloned.1.call-update) | async-done | bytes 524304 | tf_op jit(solution)/shard_map/reduce_scatter | solution.py:89
  412.1 27.6 %psum.22 = f32[256]{0:T(256)S(1)} all-reduce(f32[256]{0:T(256)S(1)} %multiply_reduce_fusion.2), channel_id=1, replica_groups=mesh['sec'=4,'dp'=8,'mp'=4] {'sec','mp'}, use_global_device_ids=true, to_apply=%region_11.12 | all-reduce | flops 256 | bytes 2048 | tf_op jit(solution)/shard_map/psum | solution.py:81
  439.7 1.9 multiply_convert_fusion
  441.8 6.5 copy.30
  448.3 7.6 %fusion.71 = f32[40,5120]{1,0:T(8,128)} fusion(bf16[5120,320]{0,1:T(8,128)(2,1)} %all-gather.5.cloned.1.call-done, bf16[320,8192]{1,0:T(8,128)(2,1)} %all-gather.7.cloned.1.call-done, bf16[40,8192]{1,0:T(8,128)(2,1)S(1)} %copy-done.7, pred[40]{0:T(512)(128)(4,1)S(1)} %iota_compare_fusion.2, f32[40,320]{1,0:T(8,128)S(1)} %convolution_add_fusion), kind=kOutput, calls=%fused_computation.107 | convolution fusion | flops 342036480 | bytes 10045480 | tf_op jit(solution)/shard_map/dot_general | solution.py:116
  456.0 21.5 %all-gather.11.cloned.1.call-done = bf16[256,8192]{1,0:T(8,128)(2,1)} async-done(((bf16[256,512]{1,0:T(8,128)(2,1)}), bf16[256,8192]{1,0:T(8,128)(2,1)}) %all-gather.11.cloned.1.call-update) | async-done | bytes 4194320 | tf_op jit(solution)/shard_map/all_gather | solution.py:76
  477.5 4.0 fusion.5
  481.5 5.8 all_gather.23
  487.6 3.5 fusion.3
  494.1 1.6 convolution_convert_fusion
  495.7 6.7 convolution_bitcast_fusion
  502.4 97.3 %all-reduce.2.cloned.1.call-done = f32[40,5120]{1,0:T(8,128)} async-done(((f32[40,5120]{1,0:T(8,128)}), f32[40,5120]{1,0:T(8,128)}) %all-reduce.2.cloned.1.call-update) | async-done | bytes 819216 | tf_op jit(solution)/shard_map/psum | solution.py:119
  599.7 1.5 reshape.226
  604.2 94.5 %reduce-scatter.8.cloned.1.call-done = f32[512,256]{0,1:T(8,128)} async-done(((f32[8192,256]{0,1:T(8,128)}), f32[512,256]{0,1:T(8,128)}) %reduce-scatter.8.cloned.1.call-update) | async-done | bytes 524304 | tf_op jit(solution)/shard_map/reduce_scatter | solution.py:89
  698.7 2.0 bitcast_add_fusion
  (103 shorter events, 14.1 us)
Async XLA Ops:
  7.2 69.2 %all-gather.5.cloned.1.call-start = ((), (), s32[]{:S(2)}) async-start(), calls=%async_computation.3 | async-start | bytes 3686400 | tf_op jit(solution)/shard_map/all_gather | solution.py:145
  7.9 3.5 copy-start.16
  7.9 3.6 copy-start.17
  7.9 148.5 %all-gather.7.cloned.1.call-start = ((), (), s32[]{:S(2)}) async-start(), calls=%async_computation.4 | async-start | bytes 5898240 | tf_op jit(solution)/shard_map/all_gather | solution.py:146
  8.7 2.8 copy-start.18
  8.7 67.7 %copy-start.5 = (bf16[40,5120]{1,0:T(8,128)(2,1)S(1)}, bf16[40,5120]{1,0:T(8,128)(2,1)}, u32[]{:S(2)}) copy-start(bf16[40,5120]{1,0:T(8,128)(2,1)} %param.16) | copy-start | bytes 1228804
  8.7 213.3 %reduce-scatter.4.cloned.1.call-start = ((), (), s32[]{:S(2)}) async-start(), calls=%async_computation.5 | async-start | bytes 1392640 | tf_op jit(solution)/shard_map/reduce_scatter | solution.py:107
  11.4 149.7 %copy-start = (f32[5,8,4,1280]{3,1,2,0:T(8,128)}, f32[5,8,4,1280]{3,1,2,0:T(8,128)S(1)}, u32[]{:S(2)}) copy-start(f32[5,8,4,1280]{3,1,2,0:T(8,128)S(1)} %copy.42) | copy-start | bytes 2457604
  79.4 82.4 %copy-start.19 = (bf16[512]{0:T(512)(128)(2,1)S(1)}, bf16[512]{0:T(512)(128)(2,1)}, u32[]{:S(2)}) copy-start(bf16[512]{0:T(512)(128)(2,1)} %param.22) | copy-start | bytes 3076
  79.4 82.5 %copy-start.8 = (bf16[2,8192]{1,0:T(2,128)(2,1)S(1)}, bf16[2,8192]{1,0:T(2,128)(2,1)}, u32[]{:S(2)}) copy-start(bf16[2,8192]{1,0:T(2,128)(2,1)} %param.27) | copy-start | bytes 98308
  79.4 82.5 %copy-start.20 = (s32[40]{0:T(128)S(1)}, s32[40]{0:T(128)}, u32[]{:S(2)}) copy-start(s32[40]{0:T(128)} %param.23) | copy-start | bytes 484
  161.1 127.0 %all-gather.9.cloned.1.call-start = ((), (), s32[]{:S(2)}) async-start(), calls=%async_computation.6 | async-start | bytes 4456448 | tf_op jit(solution)/shard_map/all_gather | solution.py:76
  252.0 158.9 %reduce-scatter.6.cloned.1.call-start = ((), (), s32[]{:S(2)}) async-start(), calls=%async_computation.7 | async-start | bytes 8912896 | tf_op jit(solution)/shard_map/reduce_scatter | solution.py:89
  257.8 6.4 copy-start.15
  264.4 39.0 %copy-start.9 = (pred[256,256]{0,1:T(8,128)(4,1)}, pred[256,256]{0,1:T(8,128)(4,1)S(1)}, u32[]{:S(2)}) copy-start(pred[256,256]{0,1:T(8,128)(4,1)S(1)} %fusion.36) | copy-start | bytes 196612
  288.1 10.2 %copy-start.4 = (bf16[256,8192]{1,0:T(8,128)(2,1)S(1)}, bf16[256,8192]{1,0:T(8,128)(2,1)}, u32[]{:S(2)}) copy-start(bf16[256,8192]{1,0:T(8,128)(2,1)} %copy.26) | copy-start | bytes 12582916
  298.2 3.6 copy-start.13
  298.2 3.6 copy-start.14
  301.8 0.6 copy-start.12
  313.0 164.4 %all-gather.11.cloned.1.call-start = ((), (), s32[]{:S(2)}) async-start(), calls=%async_computation.8 | async-start | bytes 4456448 | tf_op jit(solution)/shard_map/all_gather | solution.py:76
  441.6 158.2 %all-reduce.2.cloned.1.call-start = ((), (), s32[]{:S(2)}) async-start(), calls=%async_computation.10 | async-start | bytes 1638400 | tf_op jit(solution)/shard_map/psum | solution.py:119
  441.8 6.5 copy-start.7
  455.9 242.8 %reduce-scatter.8.cloned.1.call-start = ((), (), s32[]{:S(2)}) async-start(), calls=%async_computation.9 | async-start | bytes 8912896 | tf_op jit(solution)/shard_map/reduce_scatter | solution.py:89
  477.5 10.1 %copy-start.3 = (bf16[256,8192]{1,0:T(8,128)(2,1)S(1)}, bf16[256,8192]{1,0:T(8,128)(2,1)}, u32[]{:S(2)}) copy-start(bf16[256,8192]{1,0:T(8,128)(2,1)} %copy.30) | copy-start | bytes 12582916
  487.6 4.2 copy-start.10
  491.2 0.6 copy-start.11
  601.3 1.7 copy-start.1
  601.3 1.7 copy-start.6
  602.6 96.1 %copy-start.2 = (f32[512,256]{0,1:T(8,128)S(1)}, f32[512,256]{0,1:T(8,128)}, u32[]{:S(2)}) copy-start(f32[512,256]{0,1:T(8,128)} %reduce-scatter.6.cloned.1.call-done) | copy-start | bytes 1572868
Sparse Core Ops, SparseCore 0:
  10.4 65.9 all-gather.4
  78.6 77.7 all-gather.6
  161.2 60.7 reduce-scatter.3
  252.1 35.9 all-gather.8
  313.2 97.6 reduce-scatter.5
  441.7 35.7 all-gather.10
  480.5 119.1 all-reduce.1
  602.1 96.5 reduce-scatter.7
where the time goes:
time: 709 us; the launch traced here: 708 us
  waiting for transfers between devices  538 us (76%)
  blocking collectives  66.9 us (9%)
  matrix products  52.9 us (7%)
  local copies, waits for them, and re-layouts  24.3 us (3%)
  between operations  15.3 us (2%)
  other arithmetic  9.97 us (1%)
    reduce_scatter x2, waiting for transfers between devices, section_features(): lax.psum_scatter(lax.dot_general(o_local, attended, (((0,), (1,)), ((), (...  192 us
    psum x1, waiting for transfers between devices, merger_back(): normed_grads = lax.psum(normed_grads, ('sec', 'mp'))  97.3 us
    all_gather x1, waiting for transfers between devices, local(): lax.all_gather(w_out, 'dp', axis=1, tiled=True)  77 us
    all_gather x1, waiting for transfers between devices, local(): lax.all_gather(w_in, 'dp', axis=0, tiled=True)  64.8 us
    reduce_scatter x1, waiting for transfers between devices, merger_front(): lax.psum_scatter(partial_out, ('sec', 'mp'), scatter_dimension=1, tiled=T...  60 us
    psum x2, blocking collectives, section_features(): lax.psum(jnp.sum(rows_local * rows_local, axis=1), ('sec', 'mp'))  55.3 us
    all_gather x2, waiting for transfers between devices, gather_features(): return lax.all_gather(rows_local, ('sec', 'mp'), axis=1, tiled=True)  44.8 us
    dot_general x3, local copies, waits for them, and re-layouts, attend(): jnp.dot(normed, q_local, preferred_element_type=jnp.float32)  18.6 us
  transfers between devices with their start and end apart: 8, of which 8 were waited for; matrix products, arithmetic and copies ran while one was open for 8% of the time, Pallas kernels for 0%

commit v1 on v0

--- a/solution.py
+++ b/solution.py
@@ -3,6 +3,7 @@
 import jax.numpy as jnp
 from jax import lax
 from jax.sharding import PartitionSpec as P
+from jax.lax import all_to_all, axis_size
 
 D = 8192
 HEAD_DIM = 128
@@ -143,7 +144,7 @@
 ):
     w_in_full, w_out_full = (
         lax.all_gather(w_in, "dp", axis=0, tiled=True),
-        lax.all_gather(w_out, "dp", axis=1, tiled=True),
+        jnp.concatenate(all_to_all(jnp.stack(axis_size("dp") * [w_out], axis=0), "dp", 0, 0), 1),
     )
     slot_count = patches.shape[0]
     tokens = text_rows.shape[0]

time: 709 us -> 679 us (0.958)
  waiting for transfers between devices: 538 us -> 493 us
  local copies, waits for them, and re-layouts: 24.3 us -> 33.3 us
  starting transfers between devices: 0.5 us -> 8.49 us
    all_gather x1 -> x0, waiting for transfers between devices: 77 us -> none  [local(): lax.all_gather(w_out, 'dp', axis=1, tiled=True)]
    all_to_all x0 -> x1, waiting for transfers between devices: none -> 64.6 us  [local(): all_to_all(jnp.stack(axis_size('dp') * [w_out], axis=0), 'dp', 0, 0)]
    all_gather x1, waiting for transfers between devices: 64.8 us -> 34.2 us  [local(): lax.all_gather(w_in, 'dp', axis=0, tiled=True)]
    all_to_all x0 -> x1, starting transfers between devices: none -> 8.02 us  [local(): all_to_all(jnp.stack(axis_size('dp') * [w_out], axis=0), 'dp', 0, 0)]
  transfers between devices with their start and end apart: 8 -> 8, of which waited for: 8 -> 8; matrix products, arithmetic and copies ran while one was open for 8% -> 9% of each run, Pallas kernels for 0% -> 0%
where the time goes in v1:
time: 679 us; the launch traced here: 678 us
  waiting for transfers between devices  493 us (73%)
  blocking collectives  66.8 us (10%)
  matrix products  50.5 us (7%)
  local copies, waits for them, and re-layouts  33.3 us (5%)
  between operations  15.2 us (2%)
  other arithmetic  10.6 us (2%)
  starting transfers between devices  8.49 us (1%)
    reduce_scatter x2, waiting for transfers between devices, section_features(): lax.psum_scatter(lax.dot_general(o_local, attended, (((0,), (1,)), ((), (...  192 us
    psum x1, waiting for transfers between devices, merger_back(): normed_grads = lax.psum(normed_grads, ('sec', 'mp'))  98 us
    all_to_all x1, waiting for transfers between devices, local(): all_to_all(jnp.stack(axis_size('dp') * [w_out], axis=0), 'dp', 0, 0)  64.6 us
    reduce_scatter x1, waiting for transfers between devices, merger_front(): lax.psum_scatter(partial_out, ('sec', 'mp'), scatter_dimension=1, tiled=T...  59.3 us
    psum x2, blocking collectives, section_features(): lax.psum(jnp.sum(rows_local * rows_local, axis=1), ('sec', 'mp'))  55.3 us
    all_gather x2, waiting for transfers between devices, gather_features(): return lax.all_gather(rows_local, ('sec', 'mp'), axis=1, tiled=True)  44.8 us
    all_gather x1, waiting for transfers between devices, local(): lax.all_gather(w_in, 'dp', axis=0, tiled=True)  34.2 us
    dot_general x3, local copies, waits for them, and re-layouts, attend(): jnp.dot(normed, q_local, preferred_element_type=jnp.float32)  18.5 us
  transfers between devices with their start and end apart: 8, of which 8 were waited for; matrix products, arithmetic and copies ran while one was open for 9% of the time, Pallas kernels for 0%

profile of v1, /device:TPU:0, one launch (start us, length us, event | category | flops | bytes accessed | tf_op | source)
XLA Modules:
  0.0 678.3 jit_solution(6715559119171740778)
XLA Ops:
  7.9 4.1 stack.2
  12.0 8.0 %all-to-all-start = ((bf16[8,320,1024]{2,1,0:T(8,128)(2,1)}), bf16[8,320,1024]{2,1,0:T(8,128)(2,1)}, u32[]{:S(2)}, u32[]{:S(2)}) async-start(bf16[8,320,1024]{2,1,0:T(8,128)(2,1)} %stack.2), calls=%async_computation | async-start | bytes 10485760 | tf_op jit(solution)/shard_map/all_to_all | solution.py:147
  21.9 64.6 %all-to-all-done = bf16[8,320,1024]{2,1,0:T(8,128)(2,1)} async-done(((bf16[8,320,1024]{2,1,0:T(8,128)(2,1)}), bf16[8,320,1024]{2,1,0:T(8,128)(2,1)}, u32[]{:S(2)}, u32[]{:S(2)}) %all-to-all-start) | async-done | bytes 5242912 | tf_op jit(solution)/shard_map/all_to_all | solution.py:147
  86.5 5.7 copy.60
  92.2 34.2 %all-gather.4.cloned.1.call-done = bf16[5120,320]{0,1:T(8,128)(2,1)} async-done(((bf16[640,320]{0,1:T(8,128)(2,1)}), bf16[5120,320]{0,1:T(8,128)(2,1)}) %all-gather.4.cloned.1.call-update) | async-done | bytes 3276816 | tf_op jit(solution)/shard_map/all_gather | solution.py:146
  126.4 3.2 convolution_add_fusion
  129.9 2.2 fusion.88
  133.6 59.3 %reduce-scatter.4.cloned.1.call-done = f32[40,512]{1,0:T(8,128)} async-done(((f32[40,8192]{1,0:T(8,128)}), f32[40,512]{1,0:T(8,128)}) %reduce-scatter.4.cloned.1.call-update) | async-done | bytes 81936 | tf_op jit(solution)/shard_map/reduce_scatter | solution.py:108
  194.2 27.7 %psum.21 = f32[256]{0:T(256)S(1)} all-reduce(f32[256]{0:T(256)S(1)} %get-tuple-element.16), channel_id=1, replica_groups=mesh['sec'=4,'dp'=8,'mp'=4] {'sec','mp'}, use_global_device_ids=true, to_apply=%region_5.6 | all-reduce | flops 256 | bytes 2048 | tf_op jit(solution)/shard_map/psum | solution.py:82
  222.8 5.7 slice_bitcast_fusion.1
  228.5 6.4 copy.44
  235.5 23.4 %all-gather.6.cloned.1.call-done = bf16[256,8192]{1,0:T(8,128)(2,1)} async-done(((bf16[256,512]{1,0:T(8,128)(2,1)}), bf16[256,8192]{1,0:T(8,128)(2,1)}) %all-gather.6.cloned.1.call-update) | async-done | bytes 4194320 | tf_op jit(solution)/shard_map/all_gather | solution.py:77
  258.9 4.0 fusion.10
  262.9 5.8 all_gather.17
  269.0 3.5 fusion.8
  275.5 1.6 convolution_convert_fusion.1
  277.1 6.7 convolution_bitcast_fusion.1
  284.5 97.1 %reduce-scatter.6.cloned.1.call-done = f32[512,256]{0,1:T(8,128)} async-done(((f32[8192,256]{0,1:T(8,128)}), f32[512,256]{0,1:T(8,128)}) %reduce-scatter.6.cloned.1.call-update) | async-done | bytes 524304 | tf_op jit(solution)/shard_map/reduce_scatter | solution.py:90
  382.8 27.6 %psum.22 = f32[256]{0:T(256)S(1)} all-reduce(f32[256]{0:T(256)S(1)} %multiply_reduce_fusion.2), channel_id=1, replica_groups=mesh['sec'=4,'dp'=8,'mp'=4] {'sec','mp'}, use_global_device_ids=true, to_apply=%region_11.12 | all-reduce | flops 256 | bytes 2048 | tf_op jit(solution)/shard_map/psum | solution.py:82
  410.4 1.9 multiply_convert_fusion
  412.5 6.4 copy.48
  418.9 7.8 %fusion.71 = f32[40,5120]{1,0:T(8,128)} fusion(bf16[5120,320]{0,1:T(8,128)(2,1)} %all-gather.4.cloned.1.call-done, bf16[320,8192]{1,0:T(8,128)(2,1)} %bitcast.120, bf16[40,8192]{1,0:T(8,128)(2,1)} %param.31, pred[40]{0:T(512)(128)(4,1)S(1)} %iota_compare_fusion.2, f32[40,320]{1,0:T(8,128)S(1)} %convolution_add_fusion), kind=kOutput, calls=%fused_computation.107 | convolution fusion | flops 342036480 | bytes 10045480 | tf_op jit(solution)/shard_map/dot_general | solution.py:117
  426.8 21.4 %all-gather.8.cloned.1.call-done = bf16[256,8192]{1,0:T(8,128)(2,1)} async-done(((bf16[256,512]{1,0:T(8,128)(2,1)}), bf16[256,8192]{1,0:T(8,128)(2,1)}) %all-gather.8.cloned.1.call-update) | async-done | bytes 4194320 | tf_op jit(solution)/shard_map/all_gather | solution.py:77
  448.2 4.0 fusion.5
  452.2 5.8 all_gather.19
  458.4 3.5 fusion.3
  464.1 1.6 convolution_convert_fusion
  465.7 6.7 convolution_bitcast_fusion
  472.5 98.0 %all-reduce.2.cloned.1.call-done = f32[40,5120]{1,0:T(8,128)} async-done(((f32[40,5120]{1,0:T(8,128)}), f32[40,5120]{1,0:T(8,128)}) %all-reduce.2.cloned.1.call-update) | async-done | bytes 819216 | tf_op jit(solution)/shard_map/psum | solution.py:120
  570.5 1.5 reshape.236
  574.9 94.5 %reduce-scatter.8.cloned.1.call-done = f32[512,256]{0,1:T(8,128)} async-done(((f32[8192,256]{0,1:T(8,128)}), f32[512,256]{0,1:T(8,128)}) %reduce-scatter.8.cloned.1.call-update) | async-done | bytes 524304 | tf_op jit(solution)/shard_map/reduce_scatter | solution.py:90
  669.5 2.0 bitcast_add_fusion
  (102 shorter events, 17.2 us)
Async XLA Ops:
  7.2 119.2 %all-gather.4.cloned.1.call-start = ((), (), s32[]{:S(2)}) async-start(), calls=%async_computation.4 | async-start | bytes 3686400 | tf_op jit(solution)/shard_map/all_gather | solution.py:146
  12.0 8.1 %copy-start.6 = (bf16[40,5120]{1,0:T(8,128)(2,1)S(1)}, bf16[40,5120]{1,0:T(8,128)(2,1)}, u32[]{:S(2)}) copy-start(bf16[40,5120]{1,0:T(8,128)(2,1)} %param.16) | copy-start | bytes 1228804
  12.0 74.4 %all-to-all-start = ((bf16[8,320,1024]{2,1,0:T(8,128)(2,1)}), bf16[8,320,1024]{2,1,0:T(8,128)(2,1)}, u32[]{:S(2)}, u32[]{:S(2)}) async-start(bf16[8,320,1024]{2,1,0:T(8,128)(2,1)} %stack.2), calls=%async_computation | async-start | bytes 10485760 | tf_op jit(solution)/shard_map/all_to_all | solution.py:147
  20.0 1.7 copy-start.15
  20.0 1.8 copy-start.16
  20.0 1.8 copy-start.17
  20.1 172.8 %reduce-scatter.4.cloned.1.call-start = ((), (), s32[]{:S(2)}) async-start(), calls=%async_computation.5 | async-start | bytes 1392640 | tf_op jit(solution)/shard_map/reduce_scatter | solution.py:108
  21.8 104.6 %copy-start.1 = (f32[5,8,4,1280]{3,1,2,0:T(8,128)}, f32[5,8,4,1280]{3,1,2,0:T(8,128)S(1)}, u32[]{:S(2)}) copy-start(f32[5,8,4,1280]{3,1,2,0:T(8,128)S(1)} %copy.61) | copy-start | bytes 2457604
  126.4 3.5 copy-start
  129.9 2.9 copy-start.18
  129.9 2.9 copy-start.9
  129.9 3.6 copy-start.19
  129.9 63.0 %copy-start.8 = (bf16[256,512]{1,0:T(8,128)(2,1)S(1)}, bf16[256,512]{1,0:T(8,128)(2,1)}, u32[]{:S(2)}) copy-start(bf16[256,512]{1,0:T(8,128)(2,1)} %param.25) | copy-start | bytes 786436
  132.0 126.8 %all-gather.6.cloned.1.call-start = ((), (), s32[]{:S(2)}) async-start(), calls=%async_computation.6 | async-start | bytes 4456448 | tf_op jit(solution)/shard_map/all_gather | solution.py:77
  222.8 158.9 %reduce-scatter.6.cloned.1.call-start = ((), (), s32[]{:S(2)}) async-start(), calls=%async_computation.7 | async-start | bytes 8912896 | tf_op jit(solution)/shard_map/reduce_scatter | solution.py:90
  228.5 6.5 copy-start.14
  258.9 10.1 %copy-start.5 = (bf16[256,8192]{1,0:T(8,128)(2,1)S(1)}, bf16[256,8192]{1,0:T(8,128)(2,1)}, u32[]{:S(2)}) copy-start(bf16[256,8192]{1,0:T(8,128)(2,1)} %copy.44) | copy-start | bytes 12582916
  269.0 3.6 copy-start.13
  272.6 0.6 copy-start.10
  283.8 164.4 %all-gather.8.cloned.1.call-start = ((), (), s32[]{:S(2)}) async-start(), calls=%async_computation.8 | async-start | bytes 4456448 | tf_op jit(solution)/shard_map/all_gather | solution.py:77
  412.3 158.2 %all-reduce.2.cloned.1.call-start = ((), (), s32[]{:S(2)}) async-start(), calls=%async_computation.10 | async-start | bytes 1638400 | tf_op jit(solution)/shard_map/psum | solution.py:120
  426.8 242.7 %reduce-scatter.8.cloned.1.call-start = ((), (), s32[]{:S(2)}) async-start(), calls=%async_computation.9 | async-start | bytes 8912896 | tf_op jit(solution)/shard_map/reduce_scatter | solution.py:90
  448.2 10.2 %copy-start.4 = (bf16[256,8192]{1,0:T(8,128)(2,1)S(1)}, bf16[256,8192]{1,0:T(8,128)(2,1)}, u32[]{:S(2)}) copy-start(bf16[256,8192]{1,0:T(8,128)(2,1)} %copy.48) | copy-start | bytes 12582916
  458.3 3.6 copy-start.11
  458.4 3.6 copy-start.12
  572.0 1.7 copy-start.2
  572.0 1.7 copy-start.7
  573.4 96.1 %copy-start.3 = (f32[512,256]{0,1:T(8,128)S(1)}, f32[512,256]{0,1:T(8,128)}, u32[]{:S(2)}) copy-start(f32[512,256]{0,1:T(8,128)} %reduce-scatter.6.cloned.1.call-done) | copy-start | bytes 1572868
Sparse Core Ops, SparseCore 0:
  10.4 115.9 all-gather.3
  132.2 60.6 reduce-scatter.3
  222.9 35.9 all-gather.5
  283.9 97.6 reduce-scatter.5
  412.4 35.7 all-gather.7
  451.1 119.3 all-reduce.1
  572.9 96.5 reduce-scatter.7
